TPU v7x, 256 devices: a whole 4x4x8 slice. The times are simulated.
256 devices in a mesh: ctx: 64 (over z, x_hi, y), tp: 4 (over x_lo, core).
Axes of the slice: x: 4 (x_hi: 2, x_lo: 2; x = x_hi * 2 + x_lo), y: 4, z: 8, core: 2. Of those that a mesh axis runs over, the one named last changes fastest.
Arguments:
- query_raw: bfloat16 [32768, 2048], P('ctx', 'tp'), may hold values from -6 to 6
- key_unnormed: bfloat16 [32768, 1024], P('ctx', 'tp'), may hold values from -6 to 6
- value_matrix: bfloat16 [32768, 1024], P('ctx', 'tp'), may hold values from -6 to 6
- output_grad: bfloat16 [32768, 3840], P(('ctx', 'tp')), may hold values from -24 to 24
- output_weight: bfloat16 [3840, 2048], P('ctx', 'tp'), may hold values from -0.125 to 0.125
Outputs:
- query_grad: bfloat16 [32768, 2048], P('ctx', 'tp')
- key_raw_gradient: bfloat16 [32768, 1024], P('ctx', 'tp')
- value_rows_gradient: bfloat16 [32768, 1024], P('ctx', 'tp')
- weight_grad: float32 [3840, 2048], P('ctx', 'tp')
All inputs are finite; a program needn't handle non-finite values.
Results may differ from a plain program's by a relative error of at most 0.01.
Values may be sent and summed in bfloat16 or wider, within the bound.
No kernel may reach another device: no remote copies, remote signals or barrier semaphores. Data moves between devices by JAX's collectives and lax.ppermute only.
A program may use at most 128 MiB of HBM per device.

v0:
```python
import functools

import jax
import jax.numpy as jnp
from jax import lax
from jax.experimental import pallas as pl
from jax.experimental.pallas import tpu as pltpu
from jax.sharding import Mesh, PartitionSpec as P

HEAD_SIZE = 256
WINDOW_TOKENS = 1024
EPSILON = 1e-06
SIZES = {"z": 8, "xh": 2, "y": 4, "xl": 2, "core": 2}
CTX = ("z", "xh", "y")
TP = ("xl", "core")
F32 = jnp.float32
BF16 = jnp.bfloat16
SPAN = 512
CHUNK = 128
REACH = CHUNK + WINDOW_TOKENS
HEADS = 2
SCALE = HEAD_SIZE ** (-0.5)
ANY = pl.BlockSpec(memory_space=pl.ANY)
VMEM = pl.BlockSpec(memory_space=pltpu.VMEM)
SMEM = pl.BlockSpec(memory_space=pltpu.SMEM)


def params(micros):
    return dict(
        compiler_params=pltpu.CompilerParams(vmem_limit_bytes=48 * 2**20),
        cost_estimate=pl.CostEstimate(flops=micros * 10**9, bytes_accessed=2**20, transcendentals=0),
    )


def after(values, *others):
    return lax.optimization_barrier((values, others))[0]


def shift(block, axis, distance):
    size = SIZES[axis]
    return lax.ppermute(block, axis, [(i, (i + distance) % size) for i in range(size)])


def from_behind(block, distance):
    devices = range(SIZES["z"] * SIZES["xh"] * SIZES["y"])
    route = [(i - distance, i) for i in devices if i - distance in devices]
    return lax.ppermute(block, CTX, route)


def normalized_rows(raw):
    widened = raw.astype(F32)
    factor = lax.rsqrt(jnp.mean(widened * widened, axis=-1, keepdims=True) + EPSILON)
    return (widened * factor, factor)


def normalized_backward(grad, normed, factor):
    return factor * (grad - normed * jnp.mean(grad * normed, axis=-1, keepdims=True))


def contract(left, right, left_axis, right_axis):
    return lax.dot_general(
        left, right, (((left_axis,), (right_axis,)), ((), ())), preferred_element_type=F32
    )


def copy_all(pairs, sems):
    copies = [
        pltpu.make_async_copy(source, target, sems.at[i]) for i, (source, target) in enumerate(pairs)
    ]
    for copy in copies:
        copy.start()
    return copies


def chunk_probs(q, k, first_valid, i):
    scores = contract(q, k, 1, 1) * SCALE
    row = lax.broadcasted_iota(jnp.int32, (CHUNK, 1), 0)
    column = lax.broadcasted_iota(jnp.int32, (CHUNK, REACH), 1)
    low = jnp.maximum(row, first_valid - 1 - CHUNK * i)
    visible = (column > low) & (column <= row + WINDOW_TOKENS)
    weights = jnp.where(visible, jnp.exp(scores), 0.0)
    return weights / jnp.sum(weights, axis=1, keepdims=True)


def query_kernel(q_ref, low_ref):
    for h in range(HEADS):
        columns = slice(h * HEAD_SIZE, (h + 1) * HEAD_SIZE)
        unit, _ = normalized_rows(q_ref[:, columns])
        low_ref[:, columns] = unit.astype(BF16)


def norm_queries(query_raw):
    return pl.pallas_call(
        query_kernel,
        out_shape=jax.ShapeDtypeStruct(query_raw.shape, BF16),
        in_specs=[VMEM],
        out_specs=VMEM,
        **params(60),
    )(query_raw)


def query_grad_kernel(grad_ref, q_ref, out_ref):
    for h in range(HEADS):
        columns = slice(h * HEAD_SIZE, (h + 1) * HEAD_SIZE)
        unit, factor = normalized_rows(q_ref[:, columns])
        out_ref[:, columns] = normalized_backward(grad_ref[:, columns], unit, factor).astype(BF16)


def finish_queries(grad, query_raw):
    return pl.pallas_call(
        query_grad_kernel,
        out_shape=jax.ShapeDtypeStruct(query_raw.shape, BF16),
        in_specs=[VMEM, VMEM],
        out_specs=VMEM,
        **params(40),
    )(grad, query_raw)


def forward_kernel(place, q_ref, kv2, kv1, kv0, out_ref, keys, sems):
    copies = copy_all([(ref, keys.at[pl.ds(SPAN * n, SPAN)]) for n, ref in enumerate((kv2, kv1, kv0))], sems)
    first_valid = WINDOW_TOKENS - SPAN * place[0]
    for copy in copies:
        copy.wait()
    for i in range(SPAN // CHUNK):
        rows = slice(CHUNK * i, CHUNK * (i + 1))
        k = keys[CHUNK * i : CHUNK * i + REACH, :HEAD_SIZE]
        v = keys[CHUNK * i : CHUNK * i + REACH, HEAD_SIZE:]
        for h in range(HEADS):
            prob = chunk_probs(q_ref[rows, h * HEAD_SIZE : (h + 1) * HEAD_SIZE], k, first_valid, i)
            out_ref[rows, h * HEAD_SIZE : (h + 1) * HEAD_SIZE] = contract(
                prob.astype(BF16), v, 1, 0
            ).astype(BF16)


def attend(place, query_raw, kv2, kv1, kv0):
    return pl.pallas_call(
        forward_kernel,
        out_shape=jax.ShapeDtypeStruct((SPAN, HEADS * HEAD_SIZE), BF16),
        in_specs=[SMEM, VMEM, ANY, ANY, ANY],
        out_specs=VMEM,
        scratch_shapes=[
            pltpu.VMEM((3 * SPAN, 2 * HEAD_SIZE), BF16),
            pltpu.SemaphoreType.DMA((3,)),
        ],
        **params(15),
    )(place, query_raw, kv2, kv1, kv0)


def grad_rows(place, grads, target):
    xl, core = place[1], place[2]
    size = SPAN // 4
    spots = (xl * 2 + core, (1 - xl) * 2 + core, xl * 2 + 1 - core, (1 - xl) * 2 + 1 - core)
    return [
        (ref, target.at[pl.ds(pl.multiple_of(spot * size, size), size)])
        for ref, spot in zip(grads, spots)
    ]


def weight_kernel(place, att_ref, g0, g1, g2, g3, out_ref, grad, sems):
    copies = copy_all(grad_rows(place, (g0, g1, g2, g3), grad), sems)
    for copy in copies:
        copy.wait()
    tile = HEAD_SIZE
    for n in range(grad.shape[1] // tile):
        part = contract(grad[:, n * tile : (n + 1) * tile], att_ref[...], 0, 0)
        out_ref[n * tile : (n + 1) * tile, :] = part.astype(BF16)


def weight_partials(place, attended, grads):
    width = grads[0].shape[1]
    return pl.pallas_call(
        weight_kernel,
        out_shape=jax.ShapeDtypeStruct((width, HEADS * HEAD_SIZE), BF16),
        in_specs=[SMEM, VMEM] + [ANY] * 4,
        out_specs=VMEM,
        scratch_shapes=[pltpu.VMEM((SPAN, width), BF16), pltpu.SemaphoreType.DMA((4,))],
        **params(20),
    )(place, attended, *grads)


def backward_kernel(pieces, place, q_ref, att_ref, kv2, kv1, kv0, *refs):
    grads, refs = refs[:4], refs[4:]
    parts, refs = refs[:pieces], refs[pieces:]
    query_ref, far_ref, near_ref, own_ref, keys, grad, weight, key_sum, value_sum, sems = refs
    pairs = grad_rows(place, grads, grad) + [(parts[0], weight)]
    pairs += [(ref, keys.at[pl.ds(SPAN * n, SPAN)]) for n, ref in enumerate((kv2, kv1, kv0))]
    copies = copy_all(pairs, sems)
    key_sum[...] = jnp.zeros_like(key_sum)
    value_sum[...] = jnp.zeros_like(value_sum)
    first_valid = WINDOW_TOKENS - SPAN * place[0]
    for copy in copies:
        copy.wait()
    for i in range(SPAN // CHUNK):
        rows = slice(CHUNK * i, CHUNK * (i + 1))
        window = slice(CHUNK * i, CHUNK * i + REACH)
        k, v = keys[window, :HEAD_SIZE], keys[window, HEAD_SIZE:]
        grad_heads = contract(grad[rows, :], weight[...], 1, 0).astype(BF16)
        for h in range(HEADS):
            columns = slice(h * HEAD_SIZE, (h + 1) * HEAD_SIZE)
            q = q_ref[rows, columns]
            grad_h = grad_heads[:, columns]
            prob = chunk_probs(q, k, first_valid, i)
            delta = jnp.sum(
                grad_h.astype(F32) * att_ref[rows, columns].astype(F32), axis=1, keepdims=True
            )
            grad_prob = contract(grad_h, v, 1, 1)
            grad_score = (prob * (grad_prob - delta) * SCALE).astype(BF16)
            query_ref[rows, columns] = contract(grad_score, k, 1, 0)
            key_sum[window, :] += contract(grad_score, q, 0, 0)
            value_sum[window, :] += contract(prob.astype(BF16), grad_h, 0, 0)
    for n, ref in enumerate((far_ref, near_ref, own_ref)):
        rows = slice(SPAN * n, SPAN * (n + 1))
        ref[:, :HEAD_SIZE] = key_sum[rows, :].astype(ref.dtype)
        ref[:, HEAD_SIZE:] = value_sum[rows, :].astype(ref.dtype)


def backward(place, query_raw, attended, keys, grads, parts):
    width = grads[0].shape[1]
    both = 2 * HEAD_SIZE
    return pl.pallas_call(
        functools.partial(backward_kernel, len(parts)),
        out_shape=(
            jax.ShapeDtypeStruct((SPAN, HEADS * HEAD_SIZE), F32),
            jax.ShapeDtypeStruct((SPAN, both), BF16),
            jax.ShapeDtypeStruct((SPAN, both), BF16),
            jax.ShapeDtypeStruct((SPAN, both), F32),
        ),
        in_specs=[SMEM, VMEM, VMEM] + [ANY] * (3 + 4 + len(parts)),
        out_specs=(VMEM,) * 4,
        scratch_shapes=[
            pltpu.VMEM((3 * SPAN, both), BF16),
            pltpu.VMEM((SPAN, width), BF16),
            pltpu.VMEM((width, HEADS * HEAD_SIZE), BF16),
            pltpu.VMEM((3 * SPAN, HEAD_SIZE), F32),
            pltpu.VMEM((3 * SPAN, HEAD_SIZE), F32),
            pltpu.SemaphoreType.DMA((3 + 4 + len(parts),)),
        ],
        **params(25),
    )(place, query_raw, attended, *keys, *grads, *parts)


def gather_y(rows):
    y = lax.axis_index("y")
    w = rows[None]
    far = lax.ppermute(w, "y", [(i, i ^ 1) for i in range(4)])
    w = jnp.where(y % 2 == 0, jnp.concatenate([w, far]), jnp.concatenate([far, w]))
    far = lax.ppermute(w, "y", [(i, i ^ 2) for i in range(4)])
    w = jnp.where(y // 2 == 0, jnp.concatenate([w, far]), jnp.concatenate([far, w]))
    return w.reshape(4 * rows.shape[0], -1)


def scatter(pieces, axes):
    got = lax.all_to_all(pieces.astype(BF16), axes, 0, 0)
    return jnp.sum(got.astype(F32), axis=0)


def body(query_raw, key_unnormed, value_matrix, output_grad, output_weight):
    rows = output_weight.shape[0]
    xh = lax.axis_index("xh")
    place = jnp.stack(
        [lax.axis_index(CTX), lax.axis_index("xl"), lax.axis_index("core"), lax.axis_index("z")]
    ).astype(jnp.int32)
    key_unit, key_factor = normalized_rows(key_unnormed)
    own_keys = jnp.concatenate([key_unit.astype(BF16), value_matrix], axis=1)

    near = gather_y(output_weight)
    across = shift(near, "xh", 1)
    piece = jnp.where(xh == 0, jnp.concatenate([near, across]), jnp.concatenate([across, near]))
    own_keys, xl_source, query_raw, piece = after((own_keys, output_grad, query_raw, piece), piece)
    keys = [from_behind(own_keys, 2), from_behind(own_keys, 1), own_keys]
    xl_grad = shift(xl_source, "xl", 1)
    core_grad = shift(xl_source, "core", 1)
    weight = lax.all_gather(piece, "z", axis=0, tiled=True)
    q_norm = norm_queries(query_raw)
    core_xl_grad = shift(xl_grad, "core", 1)
    attended = attend(place, q_norm, *keys)
    grads = [output_grad, xl_grad, core_grad, core_xl_grad]
    partial = weight_partials(place, attended, grads)
    weight, q_norm = after((weight, q_norm), partial)
    partial = lax.psum_scatter(partial, "z", scatter_dimension=0, tiled=True)
    query_sum, far, close, own = backward(
        place, q_norm, attended, keys, grads, [weight]
    )
    far_got, close_got = from_behind(far, -2), from_behind(close, -1)
    query_grad = finish_queries(query_sum, query_raw)
    weight_grad = scatter(partial.reshape(8, rows, -1), ("xh", "y"))
    combined = own + close_got.astype(F32) + far_got.astype(F32)
    key_raw_gradient = normalized_backward(combined[:, :HEAD_SIZE], key_unit, key_factor).astype(BF16)
    value_rows_gradient = combined[:, HEAD_SIZE:].astype(BF16)
    return (query_grad, key_raw_gradient, value_rows_gradient, weight_grad)


def solution(mesh):
    fine = Mesh(mesh.devices.reshape(tuple(SIZES.values())), tuple(SIZES))
    split = P(CTX, TP)
    placed = (split, split, split, P(CTX + TP, None), split)
    return jax.shard_map(
        body, mesh=fine, in_specs=placed, out_specs=(split,) * 4, check_vma=False
    )
```

profile of v0, /device:TPU:2, one launch (start us, length us, event | category | flops | bytes accessed | tf_op | source)
XLA Modules:
  0.0 197.2 jit_solution(3930180826403650472)
XLA Ops:
  7.2 0.0 copy-start
  7.2 0.0 all-gather.2.cloned.1.call-start
  7.2 1.7 collective-permute-start
  8.9 1.1 fusion.7
  10.0 1.8 collective-permute-done
  11.8 0.9 maximum_select_fusion.2
  12.7 3.3 %collective-permute-start.1 = (bf16[2,60,512]{2,1,0:T(8,128)(2,1)S(1)}, bf16[2,60,512]{2,1,0:T(8,128)(2,1)S(1)}, u32[]{:S(2)}, u32[]{:S(2)}) collective-permute-start(bf16[2,60,512]{2,1,0:T(8,128)(2,1)S(1)} %maximum_select_fusion.2), channel_id=1, source_target_pairs={{0,8},{4,12},{8,0},{12,4},{1,9},{5,13},{9,1},{13,5},{2,10},{6,14},... | collective-permute-start | bytes 368648 | tf_op jit(solution)/shard_map/ppermute | solution.py:247
  16.0 3.3 %collective-permute-done.1 = bf16[2,60,512]{2,1,0:T(8,128)(2,1)S(1)} collective-permute-done((bf16[2,60,512]{2,1,0:T(8,128)(2,1)S(1)}, bf16[2,60,512]{2,1,0:T(8,128)(2,1)S(1)}, u32[]{:S(2)}, u32[]{:S(2)}) %collective-permute-start.1) | collective-permute-done | bytes 122912 | tf_op jit(solution)/shard_map/ppermute | solution.py:247
  19.3 0.1 select_n.46
  19.4 2.2 %collective-permute-start.2 = (bf16[240,512]{1,0:T(8,128)(2,1)S(1)}, bf16[240,512]{1,0:T(8,128)(2,1)S(1)}, u32[]{:S(2)}, u32[]{:S(2)}) collective-permute-start(bf16[240,512]{1,0:T(8,128)(2,1)S(1)} %select_n.46), channel_id=1, source_target_pairs={{0,16},{16,0},{1,17},{17,1},{2,18},{18,2},{3,19},{19,3},{4,20},{20... | collective-permute-start | bytes 737288 | tf_op jit(solution)/shard_map/ppermute | solution.py:41
  21.6 1.1 fusion.2
  22.7 0.0 copy-done.12
  22.7 0.1 pad_add_fusion.place
  22.8 1.0 pad_maximum_fusion.kv0
  23.8 3.4 %collective-permute-done.2 = bf16[240,512]{1,0:T(8,128)(2,1)S(1)} collective-permute-done((bf16[240,512]{1,0:T(8,128)(2,1)S(1)}, bf16[240,512]{1,0:T(8,128)(2,1)S(1)}, u32[]{:S(2)}, u32[]{:S(2)}) %collective-permute-start.2) | collective-permute-done | bytes 245792 | tf_op jit(solution)/shard_map/ppermute | solution.py:41
  27.2 1.0 maximum_select_fusion
  28.2 4.3 %collective-permute-start.4 = (bf16[512,512]{1,0:T(8,128)(2,1)S(1)}, bf16[512,512]{1,0:T(8,128)(2,1)}, u32[]{:S(2)}, u32[]{:S(2)}) collective-permute-start(bf16[512,512]{1,0:T(8,128)(2,1)S(1)} %pad_maximum_fusion.kv0), channel_id=1, source_target_pairs={{0,4},{4,8},{8,12},{12,16},{16,20},{20,24},{24,28},{28,32},{32,36}... | collective-permute-start | bytes 1572872 | tf_op jit(solution)/shard_map/ppermute | solution.py:47
  32.5 4.8 %collective-permute-start.3 = (bf16[512,512]{1,0:T(8,128)(2,1)S(1)}, bf16[512,512]{1,0:T(8,128)(2,1)}, u32[]{:S(2)}, u32[]{:S(2)}) collective-permute-start(bf16[512,512]{1,0:T(8,128)(2,1)S(1)} %pad_maximum_fusion.kv0), channel_id=1, source_target_pairs={{0,8},{4,12},{8,16},{12,20},{16,24},{20,28},{24,32},{28,36},{32,40... | collective-permute-start | bytes 1572872 | tf_op jit(solution)/shard_map/ppermute | solution.py:47
  37.3 0.0 copy-done
  37.3 0.0 collective-permute-start.6
  37.3 0.5 collective-permute-start.5
  37.8 0.0 all-gather.2.cloned.1.call-update
  37.8 0.0 reduce-scatter.2.cloned.1.call-start
  37.9 0.0 copy-start.3
  37.9 1.0 copy-done.3
  38.9 0.2 shard_map.84.q_ref
  39.2 0.0 copy-start.5
  39.2 22.3 %collective-permute-done.5.g1.refs_1_ = bf16[128,3840]{1,0:T(8,128)(2,1)S(1)} collective-permute-done((bf16[128,3840]{1,0:T(8,128)(2,1)S(1)}, bf16[128,3840]{1,0:T(8,128)(2,1)S(1)}, u32[]{:S(2)}, u32[]{:S(2)}) %collective-permute-start.5) | collective-permute-done | bytes 983072 | tf_op jit(solution)/shard_map/ppermute | solution.py:41
  61.4 0.0 collective-permute-start.7
  61.5 0.0 collective-permute-done.4.kv1
  61.5 0.0 collective-permute-done.3.kv2
  61.5 5.8 %shard_map.85.att_ref = bf16[512,512]{1,0:T(8,128)(2,1)S(1)} custom-call(s32[4]{0:T(128)S(1)} %pad_add_fusion.place, bf16[512,512]{1,0:T(8,128)(2,1)S(1)} %shard_map.84.q_ref, bf16[512,512]{1,0:T(8,128)(2,1)} %collective-permute-done.3.kv2, bf16[512,512]{1,0:T(8,128)(2,1)} %collective-permute-done.4.kv1, bf16[512,512]{1,0:T(8,128)(2,1)S(1)} %pad_maximum_fusion.kv0), custom_call_target="tpu_custom_call" | custom-call | flops 15000000512 | bytes 1048576 | tf_op jit(solution)/shard_map/pallas_call | solution.py:136
  67.2 0.0 copy-done.5
  67.2 0.0 collective-permute-done.6.g2.refs_2_
  67.3 0.0 collective-permute-done.7.g3.refs_3_
  67.3 5.9 %shard_map.86 = bf16[3840,512]{1,0:T(8,128)(2,1)} custom-call(s32[4]{0:T(128)S(1)} %pad_add_fusion.place, bf16[512,512]{1,0:T(8,128)(2,1)S(1)} %shard_map.85.att_ref, bf16[128,3840]{1,0:T(8,128)(2,1)S(1)} %copy-done, bf16[128,3840]{1,0:T(8,128)(2,1)S(1)} %collective-permute-done.5.g1.refs_1_, bf16[128,3840]{1,0:T(8,128)(2,1)S(1)} %collective-permute-done.6.g2.refs_2_, ...), custom_call_target="tpu_custom_call" | custom-call | flops 20000000000 | bytes 1048576 | tf_op jit(solution)/shard_map/pallas_call | solution.py:171
  73.2 0.0 copy-done.1
  73.2 0.0 copy-start.2
  73.2 0.9 copy-done.2
  74.2 0.8 copy-done.7
  75.0 0.0 reduce-scatter.2.cloned.1.call-update
  75.0 0.0 copy-start.4
  75.0 17.8 %all-gather.2.cloned.1.call-done.refs_4_ = bf16[3840,512]{1,0:T(8,128)(2,1)} async-done(((bf16[480,512]{1,0:T(8,128)(2,1)}), bf16[3840,512]{1,0:T(8,128)(2,1)}) %all-gather.2.cloned.1.call-update) | async-done | bytes 3932176 | tf_op jit(solution)/shard_map/all_gather | solution.py:273
  92.8 1.0 copy-done.6
  93.9 1.0 copy-done.8
  94.9 14.6 %shard_map.87 = (f32[512,512]{1,0:T(8,128)}, bf16[512,512]{1,0:T(8,128)(2,1)S(1)}, bf16[512,512]{1,0:T(8,128)(2,1)S(1)}, f32[512,512]{1,0:T(8,128)}) custom-call(s32[4]{0:T(128)S(1)} %pad_add_fusion.place, bf16[512,512]{1,0:T(8,128)(2,1)S(1)} %copy-done.6, bf16[512,512]{1,0:T(8,128)(2,1)S(1)} %copy-done.8, bf16[512,512]{1,0:T(8,128)(2,1)} %collective-permute-done.3.kv2, ...), custom_call_target="tpu_custom_call" | custom-call | flops 24999999488 | bytes 1048576 | tf_op jit(solution)/shard_map/pallas_call | solution.py:220
  109.5 1.3 collective-permute-start.8
  110.8 1.3 collective-permute-start.9
  112.1 0.0 copy-done.4
  112.2 0.0 copy-start.9
  112.2 1.2 copy-done.9
  113.4 1.2 shard_map.88
  114.6 16.8 %collective-permute-done.8 = bf16[512,512]{1,0:T(8,128)(2,1)S(1)} collective-permute-done((bf16[512,512]{1,0:T(8,128)(2,1)S(1)}, bf16[512,512]{1,0:T(8,128)(2,1)S(1)}, u32[]{:S(2)}, u32[]{:S(2)}) %collective-permute-start.8) | collective-permute-done | bytes 524320 | tf_op jit(solution)/shard_map/ppermute | solution.py:47
  131.4 0.0 collective-permute-done.9
  131.4 0.2 convert_add_fusion
  131.6 0.7 slice.14
  132.3 0.0 copy-done.10
  132.3 0.2 fusion.3
  132.6 40.4 %reduce-scatter.2.cloned.1.call-done = bf16[480,512]{1,0:T(8,128)(2,1)} async-done(((bf16[3840,512]{1,0:T(8,128)(2,1)}), bf16[480,512]{1,0:T(8,128)(2,1)}) %reduce-scatter.2.cloned.1.call-update) | async-done | bytes 491536 | tf_op jit(solution)/shard_map/reduce_scatter | solution.py:280
  173.0 1.9 reshape.28
  174.9 3.5 %all-to-all-start = ((bf16[8,60,512]{2,1,0:T(8,128)(2,1)}), bf16[8,60,512]{2,1,0:T(8,128)(2,1)S(1)}, u32[]{:S(2)}, u32[]{:S(2)}) async-start(bf16[8,60,512]{2,1,0:T(8,128)(2,1)} %reshape.28), calls=%async_computation.1 | async-start | bytes 1048576 | tf_op jit(solution)/shard_map/all_to_all | solution.py:253
  178.4 0.9 fusion.6
  179.4 10.3 %all-to-all-done = bf16[8,60,512]{2,1,0:T(8,128)(2,1)S(1)} async-done(((bf16[8,60,512]{2,1,0:T(8,128)(2,1)}), bf16[8,60,512]{2,1,0:T(8,128)(2,1)S(1)}, u32[]{:S(2)}, u32[]{:S(2)}) %all-to-all-start) | async-done | bytes 491552 | tf_op jit(solution)/shard_map/all_to_all | solution.py:253
  189.6 0.7 convert_reduce_fusion
  (13 shorter events, 0.1 us)
Async XLA Ops:
  7.2 30.1 %copy-start = (bf16[128,3840]{1,0:T(8,128)(2,1)S(1)}, bf16[128,3840]{1,0:T(8,128)(2,1)}, u32[]{:S(2)}) copy-start(bf16[128,3840]{1,0:T(8,128)(2,1)} %refs_0_.1) | copy-start | bytes 2949124
  7.2 85.6 %all-gather.2.cloned.1.call-start = ((), (), s32[]{:S(2)}) async-start(), calls=%async_computation.2 | async-start | bytes 4423680 | tf_op jit(solution)/shard_map/all_gather | solution.py:273
  7.2 4.6 %collective-permute-start = (bf16[1,60,512]{2,1,0:T(8,128)(2,1)}, bf16[1,60,512]{2,1,0:T(8,128)(2,1)S(1)}, u32[]{:S(2)}, u32[]{:S(2)}) collective-permute-start(bf16[1,60,512]{2,1,0:T(8,128)(2,1)} %bitcast.5), channel_id=1, source_target_pairs={{0,4},{4,0},{8,12},{12,8},{1,5},{5,1},{9,13},{13,9},{2,6},{6,2},{1... | collective-permute-start | bytes 184328 | tf_op jit(solution)/shard_map/ppermute | solution.py:245
  12.7 6.6 %collective-permute-start.1 = (bf16[2,60,512]{2,1,0:T(8,128)(2,1)S(1)}, bf16[2,60,512]{2,1,0:T(8,128)(2,1)S(1)}, u32[]{:S(2)}, u32[]{:S(2)}) collective-permute-start(bf16[2,60,512]{2,1,0:T(8,128)(2,1)S(1)} %maximum_select_fusion.2), channel_id=1, source_target_pairs={{0,8},{4,12},{8,0},{12,4},{1,9},{5,13},{9,1},{13,5},{2,10},{6,14},... | collective-permute-start | bytes 368648 | tf_op jit(solution)/shard_map/ppermute | solution.py:247
  16.0 6.7 %copy-start.12 = (f32[512]{0:T(512)}, f32[512]{0:T(512)S(1)}, u32[]{:S(2)}) copy-start(f32[512]{0:T(512)S(1)} %add_rsqrt_fusion) | copy-start | bytes 6148
  19.4 7.8 %collective-permute-start.2 = (bf16[240,512]{1,0:T(8,128)(2,1)S(1)}, bf16[240,512]{1,0:T(8,128)(2,1)S(1)}, u32[]{:S(2)}, u32[]{:S(2)}) collective-permute-start(bf16[240,512]{1,0:T(8,128)(2,1)S(1)} %select_n.46), channel_id=1, source_target_pairs={{0,16},{16,0},{1,17},{17,1},{2,18},{18,2},{3,19},{19,3},{4,20},{20... | collective-permute-start | bytes 737288 | tf_op jit(solution)/shard_map/ppermute | solution.py:41
  28.2 33.3 %collective-permute-start.4 = (bf16[512,512]{1,0:T(8,128)(2,1)S(1)}, bf16[512,512]{1,0:T(8,128)(2,1)}, u32[]{:S(2)}, u32[]{:S(2)}) collective-permute-start(bf16[512,512]{1,0:T(8,128)(2,1)S(1)} %pad_maximum_fusion.kv0), channel_id=1, source_target_pairs={{0,4},{4,8},{8,12},{12,16},{16,20},{20,24},{24,28},{28,32},{32,36}... | collective-permute-start | bytes 1572872 | tf_op jit(solution)/shard_map/ppermute | solution.py:47
  32.5 29.0 %collective-permute-start.3 = (bf16[512,512]{1,0:T(8,128)(2,1)S(1)}, bf16[512,512]{1,0:T(8,128)(2,1)}, u32[]{:S(2)}, u32[]{:S(2)}) collective-permute-start(bf16[512,512]{1,0:T(8,128)(2,1)S(1)} %pad_maximum_fusion.kv0), channel_id=1, source_target_pairs={{0,8},{4,12},{8,16},{12,20},{16,24},{20,28},{24,32},{28,36},{32,40... | collective-permute-start | bytes 1572872 | tf_op jit(solution)/shard_map/ppermute | solution.py:47
  37.3 30.0 %collective-permute-start.6 = (bf16[128,3840]{1,0:T(8,128)(2,1)S(1)}, bf16[128,3840]{1,0:T(8,128)(2,1)S(1)}, u32[]{:S(2)}, u32[]{:S(2)}) collective-permute-start(bf16[128,3840]{1,0:T(8,128)(2,1)S(1)} %copy-done), channel_id=1, source_target_pairs={{0,1},{1,0},{2,3},{3,2},{4,5},{5,4},{6,7},{7,6},{8,9},{9,8},{10,11... | collective-permute-start | bytes 2949128 | tf_op jit(solution)/shard_map/ppermute | solution.py:41
  37.3 24.2 %collective-permute-start.5 = (bf16[128,3840]{1,0:T(8,128)(2,1)S(1)}, bf16[128,3840]{1,0:T(8,128)(2,1)S(1)}, u32[]{:S(2)}, u32[]{:S(2)}) collective-permute-start(bf16[128,3840]{1,0:T(8,128)(2,1)S(1)} %copy-done), channel_id=1, source_target_pairs={{0,2},{2,0},{1,3},{3,1},{4,6},{6,4},{5,7},{7,5},{8,10},{10,8},{9,1... | collective-permute-start | bytes 2949128 | tf_op jit(solution)/shard_map/ppermute | solution.py:41
  37.8 135.2 %reduce-scatter.2.cloned.1.call-start = ((), (), s32[]{:S(2)}) async-start(), calls=%async_computation.3 | async-start | bytes 4423680 | tf_op jit(solution)/shard_map/reduce_scatter | solution.py:280
  37.9 1.0 copy-start.3
  39.2 28.1 %copy-start.5 = (bf16[512,512]{1,0:T(8,128)(2,1)}, bf16[512,512]{1,0:T(8,128)(2,1)S(1)}, u32[]{:S(2)}) copy-start(bf16[512,512]{1,0:T(8,128)(2,1)S(1)} %shard_map.84.q_ref) | copy-start | bytes 1572868
  61.4 5.8 %collective-permute-start.7 = (bf16[128,3840]{1,0:T(8,128)(2,1)S(1)}, bf16[128,3840]{1,0:T(8,128)(2,1)S(1)}, u32[]{:S(2)}, u32[]{:S(2)}) collective-permute-start(bf16[128,3840]{1,0:T(8,128)(2,1)S(1)} %collective-permute-done.5.g1.refs_1_), channel_id=1, source_target_pairs={{0,1},{1,0},{2,3},{3,2},{4,5},{5,4},{6,7},{7,6},{8,9},{9,8},{10,11... | collective-permute-start | bytes 2949128 | tf_op jit(solution)/shard_map/ppermute | solution.py:41
  67.3 5.9 %copy-start.1 = (bf16[128,3840]{1,0:T(8,128)(2,1)}, bf16[128,3840]{1,0:T(8,128)(2,1)S(1)}, u32[]{:S(2)}) copy-start(bf16[128,3840]{1,0:T(8,128)(2,1)S(1)} %collective-permute-done.6.g2.refs_2_) | copy-start | bytes 2949124
  73.2 1.0 copy-start.2
  74.2 0.8 copy-start.7
  75.0 37.1 %copy-start.4 = (bf16[512,512]{1,0:T(8,128)(2,1)S(1)}, bf16[512,512]{1,0:T(8,128)(2,1)}, u32[]{:S(2)}) copy-start(bf16[512,512]{1,0:T(8,128)(2,1)} %q_ref.1) | copy-start | bytes 1572868
  92.8 1.0 copy-start.6
  93.9 1.0 copy-start.8
  109.5 21.8 %collective-permute-start.8 = (bf16[512,512]{1,0:T(8,128)(2,1)S(1)}, bf16[512,512]{1,0:T(8,128)(2,1)S(1)}, u32[]{:S(2)}, u32[]{:S(2)}) collective-permute-start(bf16[512,512]{1,0:T(8,128)(2,1)S(1)} %get-tuple-element.22), channel_id=1, source_target_pairs={{4,0},{8,4},{12,8},{16,12},{20,16},{24,20},{28,24},{32,28},{36,32}... | collective-permute-start | bytes 1572872 | tf_op jit(solution)/shard_map/ppermute | solution.py:47
  110.8 20.5 %collective-permute-start.9 = (bf16[512,512]{1,0:T(8,128)(2,1)S(1)}, bf16[512,512]{1,0:T(8,128)(2,1)S(1)}, u32[]{:S(2)}, u32[]{:S(2)}) collective-permute-start(bf16[512,512]{1,0:T(8,128)(2,1)S(1)} %get-tuple-element.23), channel_id=1, source_target_pairs={{8,0},{12,4},{16,8},{20,12},{24,16},{28,20},{32,24},{36,28},{40,32... | collective-permute-start | bytes 1572872 | tf_op jit(solution)/shard_map/ppermute | solution.py:47
  112.2 1.2 copy-start.9
  113.4 18.0 %copy-start.11 = (f32[512,512]{1,0:T(8,128)S(1)}, f32[512,512]{1,0:T(8,128)}, u32[]{:S(2)}) copy-start(f32[512,512]{1,0:T(8,128)} %get-tuple-element.21) | copy-start | bytes 3145732
  113.4 18.9 %copy-start.10 = (bf16[512,256]{1,0:T(8,128)(2,1)S(1)}, bf16[512,256]{1,0:T(8,128)(2,1)}, u32[]{:S(2)}) copy-start(bf16[512,256]{1,0:T(8,128)(2,1)} %param.6) | copy-start | bytes 786436
  113.4 18.9 %copy-start.13 = (f32[512]{0:T(512)S(1)}, f32[512]{0:T(512)}, u32[]{:S(2)}) copy-start(f32[512]{0:T(512)} %copy-done.12) | copy-start | bytes 6148
  174.9 14.7 %all-to-all-start = ((bf16[8,60,512]{2,1,0:T(8,128)(2,1)}), bf16[8,60,512]{2,1,0:T(8,128)(2,1)S(1)}, u32[]{:S(2)}, u32[]{:S(2)}) async-start(bf16[8,60,512]{2,1,0:T(8,128)(2,1)} %reshape.28), calls=%async_computation.1 | async-start | bytes 1048576 | tf_op jit(solution)/shard_map/all_to_all | solution.py:253
Sparse Core Ops, SparseCore 0:
  38.0 54.8 all-gather.1
  95.4 77.5 reduce-scatter.1
where the time goes:
time: 198 us; the launch traced here: 197 us
  waiting for transfers between devices  116 us (59%)
  Pallas kernels  27.8 us (14%)
  starting transfers between devices  22.9 us (12%)
  between operations  14.3 us (7%)
  local copies, waits for them, and re-layouts  8.87 us (4%)
  other arithmetic  7.31 us (4%)
    reduce_scatter x1, waiting for transfers between devices, body(): partial = lax.psum_scatter(partial, 'z', scatter_dimension=0, tiled=True)  40.4 us
    ppermute x4, waiting for transfers between devices, shift(): lax.ppermute(block, axis, [(i, (i + distance) % size) for i in range(size)])  25.7 us
    all_gather x1, waiting for transfers between devices, body(): weight = lax.all_gather(piece, 'z', axis=0, tiled=True)  17.8 us
    ppermute x4, waiting for transfers between devices, from_behind(): return lax.ppermute(block, CTX, route)  16.8 us
    pallas_call x1, Pallas kernels, backward(): pl.pallas_call(functools.partial(backward_kernel, len(parts)), out_shape=...  14.6 us
    ppermute x4, starting transfers between devices, from_behind(): return lax.ppermute(block, CTX, route)  11.7 us
    all_to_all x1, waiting for transfers between devices, scatter(): got = lax.all_to_all(pieces.astype(BF16), axes, 0, 0)  10.3 us
    unnamed x28, local copies, waits for them, and re-layouts  6.16 us
  transfers between devices with their start and end apart: 13, of which 8 were waited for; matrix products, arithmetic and copies ran while one was open for 3% of the time, Pallas kernels for 14%

commit v1 on v0

--- a/solution.py
+++ b/solution.py
@@ -188,7 +188,21 @@
     key_sum[...] = jnp.zeros_like(key_sum)
     value_sum[...] = jnp.zeros_like(value_sum)
     first_valid = WINDOW_TOKENS - SPAN * place[0]
-    for copy in copies:
+    for copy in copies[-3:]:
+        copy.wait()
+    probs = [
+        [
+            chunk_probs(
+                q_ref[CHUNK * i : CHUNK * (i + 1), h * HEAD_SIZE : (h + 1) * HEAD_SIZE],
+                keys[CHUNK * i : CHUNK * i + REACH, :HEAD_SIZE],
+                first_valid,
+                i,
+            )
+            for h in range(HEADS)
+        ]
+        for i in range(SPAN // CHUNK)
+    ]
+    for copy in copies[:-3]:
         copy.wait()
     for i in range(SPAN // CHUNK):
         rows = slice(CHUNK * i, CHUNK * (i + 1))
@@ -199,7 +213,7 @@
             columns = slice(h * HEAD_SIZE, (h + 1) * HEAD_SIZE)
             q = q_ref[rows, columns]
             grad_h = grad_heads[:, columns]
-            prob = chunk_probs(q, k, first_valid, i)
+            prob = probs[i][h]
             delta = jnp.sum(
                 grad_h.astype(F32) * att_ref[rows, columns].astype(F32), axis=1, keepdims=True
             )
@@ -239,16 +253,6 @@
     )(place, query_raw, attended, *keys, *grads, *parts)
 
 
-def gather_y(rows):
-    y = lax.axis_index("y")
-    w = rows[None]
-    far = lax.ppermute(w, "y", [(i, i ^ 1) for i in range(4)])
-    w = jnp.where(y % 2 == 0, jnp.concatenate([w, far]), jnp.concatenate([far, w]))
-    far = lax.ppermute(w, "y", [(i, i ^ 2) for i in range(4)])
-    w = jnp.where(y // 2 == 0, jnp.concatenate([w, far]), jnp.concatenate([far, w]))
-    return w.reshape(4 * rows.shape[0], -1)
-
-
 def scatter(pieces, axes):
     got = lax.all_to_all(pieces.astype(BF16), axes, 0, 0)
     return jnp.sum(got.astype(F32), axis=0)
@@ -263,13 +267,15 @@
     key_unit, key_factor = normalized_rows(key_unnormed)
     own_keys = jnp.concatenate([key_unit.astype(BF16), value_matrix], axis=1)
 
-    near = gather_y(output_weight)
-    across = shift(near, "xh", 1)
-    piece = jnp.where(xh == 0, jnp.concatenate([near, across]), jnp.concatenate([across, near]))
-    own_keys, xl_source, query_raw, piece = after((own_keys, output_grad, query_raw, piece), piece)
-    keys = [from_behind(own_keys, 2), from_behind(own_keys, 1), own_keys]
+    core_grad = shift(output_grad, "core", 1)
+    spread = jnp.broadcast_to(output_weight, (8,) + output_weight.shape)
+    piece = lax.all_to_all(spread, ("xh", "y"), 0, 0).reshape(8 * rows, -1)
+    core_grad, xl_source, piece = after((core_grad, output_grad, piece), piece, core_grad)
+    own_keys, query_raw = after((own_keys, query_raw), piece)
     xl_grad = shift(xl_source, "xl", 1)
-    core_grad = shift(xl_source, "core", 1)
+    behind = from_behind(own_keys, 1)
+    keys = [from_behind(behind, 1), behind, own_keys]
+    xl_grad = after(xl_grad, keys[0])
     weight = lax.all_gather(piece, "z", axis=0, tiled=True)
     q_norm = norm_queries(query_raw)
     core_xl_grad = shift(xl_grad, "core", 1)
@@ -281,10 +287,12 @@
     query_sum, far, close, own = backward(
         place, q_norm, attended, keys, grads, [weight]
     )
-    far_got, close_got = from_behind(far, -2), from_behind(close, -1)
+    passed_on = from_behind(far, -1).astype(F32) + close.astype(F32)
+    passed_on = from_behind(passed_on.astype(BF16), -1)
     query_grad = finish_queries(query_sum, query_raw)
     weight_grad = scatter(partial.reshape(8, rows, -1), ("xh", "y"))
-    combined = own + close_got.astype(F32) + far_got.astype(F32)
+    passed_on = after(passed_on, weight_grad)
+    combined = own + passed_on.astype(F32)
     key_raw_gradient = normalized_backward(combined[:, :HEAD_SIZE], key_unit, key_factor).astype(BF16)
     value_rows_gradient = combined[:, HEAD_SIZE:].astype(BF16)
     return (query_grad, key_raw_gradient, value_rows_gradient, weight_grad)

time: 198 us -> 194 us (0.980)
  waiting for transfers between devices: 116 us -> 110 us
  local copies, waits for them, and re-layouts: 8.87 us -> 13.1 us
    ppermute x4 -> x3, waiting for transfers between devices: 25.7 us -> 7.24 us  [shift(): lax.ppermute(block, axis, [(i, (i + distance) % size) for i in range(size)])]
    all_to_all x0 -> x1, waiting for transfers between devices: none -> 7.72 us  [body(): piece = lax.all_to_all(spread, ('xh', 'y'), 0, 0).reshape(8 * rows, -1)]
    ppermute x4, waiting for transfers between devices: 16.8 us -> 23.9 us  [from_behind(): return lax.ppermute(block, CTX, route)]
    all_to_all x0 -> x1, starting transfers between devices: none -> 6.03 us  [body(): piece = lax.all_to_all(spread, ('xh', 'y'), 0, 0).reshape(8 * rows, -1)]
    ppermute x2 -> x0, waiting for transfers between devices: 5.05 us -> none  [the longest x1 3.27 us: gather_y(): far = lax.ppermute(w, 'y', [(i, i ^ 2) for i in range(4)])]
    ppermute x2 -> x0, starting transfers between devices: 4.94 us -> none  [the longest x1 3.28 us: gather_y(): far = lax.ppermute(w, 'y', [(i, i ^ 2) for i in range(4)])]
    reduce_scatter x1, waiting for transfers between devices: 40.4 us -> 44.5 us  [body(): partial = lax.psum_scatter(partial, 'z', scatter_dimension=0, tiled=True)]
    select_n x3 -> x0, other arithmetic: 1.99 us -> none  [the longest x1 1.02 us: body(): jnp.where(xh == 0, jnp.concatenate([near, across]), jnp.concatenate([acro...]
  transfers between devices with their start and end apart: 13 -> 11, of which waited for: 8 -> 8; matrix products, arithmetic and copies ran while one was open for 3% -> 5% of each run, Pallas kernels for 14% -> 14%
where the time goes in v1:
time: 194 us; the launch traced here: 192 us
  waiting for transfers between devices  110 us (57%)
  Pallas kernels  27.3 us (14%)
  starting transfers between devices  21 us (11%)
  between operations  14.3 us (7%)
  local copies, waits for them, and re-layouts  13.1 us (7%)
  other arithmetic  6.21 us (3%)
    reduce_scatter x1, waiting for transfers between devices, body(): partial = lax.psum_scatter(partial, 'z', scatter_dimension=0, tiled=True)  44.5 us
    ppermute x4, waiting for transfers between devices, from_behind(): return lax.ppermute(block, CTX, route)  23.9 us
    all_gather x1, waiting for transfers between devices, body(): weight = lax.all_gather(piece, 'z', axis=0, tiled=True)  18.2 us
    pallas_call x1, Pallas kernels, backward(): pl.pallas_call(functools.partial(backward_kernel, len(parts)), out_shape=...  14.2 us
    ppermute x4, starting transfers between devices, from_behind(): return lax.ppermute(block, CTX, route)  9.83 us
    all_to_all x1, waiting for transfers between devices, scatter(): got = lax.all_to_all(pieces.astype(BF16), axes, 0, 0)  8.51 us
    unnamed x32, local copies, waits for them, and re-layouts  7.84 us
    all_to_all x1, waiting for transfers between devices, body(): piece = lax.all_to_all(spread, ('xh', 'y'), 0, 0).reshape(8 * rows, -1)  7.72 us
  transfers between devices with their start and end apart: 11, of which 8 were waited for; matrix products, arithmetic and copies ran while one was open for 5% of the time, Pallas kernels for 14%

profile of v1, /device:TPU:2, one launch (start us, length us, event | category | flops | bytes accessed | tf_op | source)
XLA Modules:
  0.0 191.9 jit_solution(410260871433170614)
XLA Ops:
  7.2 0.0 copy-start
  7.2 0.1 collective-permute-start
  7.3 1.7 broadcast_in_dim.2
  9.0 6.0 %all-to-all-start = ((bf16[8,60,512]{2,1,0:T(8,128)(2,1)}), bf16[8,60,512]{2,1,0:T(8,128)(2,1)S(1)}, u32[]{:S(2)}, u32[]{:S(2)}) async-start(bf16[8,60,512]{2,1,0:T(8,128)(2,1)} %broadcast_in_dim.2), calls=%async_computation | async-start | bytes 1048576 | tf_op jit(solution)/shard_map/all_to_all | solution.py:272
  15.0 0.0 all-gather.2.cloned.1.call-start
  15.1 1.1 fusion.7
  16.2 0.0 copy-start.14
  16.2 0.6 copy-done.14
  16.8 1.1 fusion.2
  17.9 1.0 pad_maximum_fusion.kv0
  18.9 7.7 %all-to-all-done = bf16[8,60,512]{2,1,0:T(8,128)(2,1)S(1)} async-done(((bf16[8,60,512]{2,1,0:T(8,128)(2,1)}), bf16[8,60,512]{2,1,0:T(8,128)(2,1)S(1)}, u32[]{:S(2)}, u32[]{:S(2)}) %all-to-all-start) | async-done | bytes 491552 | tf_op jit(solution)/shard_map/all_to_all | solution.py:272
  26.6 0.9 reshape.26
  27.5 0.0 collective-permute-done.g2.refs_2_
  27.5 2.8 %collective-permute-start.1 = (bf16[512,512]{1,0:T(8,128)(2,1)S(1)}, bf16[512,512]{1,0:T(8,128)(2,1)}, u32[]{:S(2)}, u32[]{:S(2)}) collective-permute-start(bf16[512,512]{1,0:T(8,128)(2,1)S(1)} %pad_maximum_fusion.kv0), channel_id=1, source_target_pairs={{0,4},{4,8},{8,12},{12,16},{16,20},{20,24},{24,28},{28,32},{32,36}... | collective-permute-start | bytes 1572872 | tf_op jit(solution)/shard_map/ppermute | solution.py:47
  30.2 0.1 pad_add_fusion.place
  30.3 0.0 all-gather.2.cloned.1.call-update
  30.3 0.0 reduce-scatter.2.cloned.1.call-start
  30.4 0.0 copy-done
  30.4 1.5 collective-permute-start.3
  31.9 8.2 %collective-permute-done.1.kv1 = bf16[512,512]{1,0:T(8,128)(2,1)} collective-permute-done((bf16[512,512]{1,0:T(8,128)(2,1)S(1)}, bf16[512,512]{1,0:T(8,128)(2,1)}, u32[]{:S(2)}, u32[]{:S(2)}) %collective-permute-start.1) | collective-permute-done | bytes 524320 | tf_op jit(solution)/shard_map/ppermute | solution.py:47
  40.1 4.5 %collective-permute-start.2 = (bf16[512,512]{1,0:T(8,128)(2,1)}, bf16[512,512]{1,0:T(8,128)(2,1)S(1)}, u32[]{:S(2)}, u32[]{:S(2)}) collective-permute-start(bf16[512,512]{1,0:T(8,128)(2,1)} %collective-permute-done.1.kv1), channel_id=1, source_target_pairs={{0,4},{4,8},{8,12},{12,16},{16,20},{20,24},{24,28},{28,32},{32,36}... | collective-permute-start | bytes 1572872 | tf_op jit(solution)/shard_map/ppermute | solution.py:47
  44.6 0.0 copy-start.3
  44.6 1.1 copy-done.3
  45.7 0.2 shard_map.84.q_ref
  45.9 0.0 copy-start.7
  45.9 7.2 %collective-permute-done.3.g1.refs_1_ = bf16[128,3840]{1,0:T(8,128)(2,1)S(1)} collective-permute-done((bf16[128,3840]{1,0:T(8,128)(2,1)S(1)}, bf16[128,3840]{1,0:T(8,128)(2,1)S(1)}, u32[]{:S(2)}, u32[]{:S(2)}) %collective-permute-start.3) | collective-permute-done | bytes 983072 | tf_op jit(solution)/shard_map/ppermute | solution.py:41
  53.2 1.4 collective-permute-done.2.kv2
  54.6 0.0 collective-permute-start.4
  54.6 5.6 %shard_map.85.att_ref = bf16[512,512]{1,0:T(8,128)(2,1)S(1)} custom-call(s32[4]{0:T(128)S(1)} %pad_add_fusion.place, bf16[512,512]{1,0:T(8,128)(2,1)S(1)} %shard_map.84.q_ref, bf16[512,512]{1,0:T(8,128)(2,1)S(1)} %collective-permute-done.2.kv2, bf16[512,512]{1,0:T(8,128)(2,1)} %collective-permute-done.1.kv1, bf16[512,512]{1,0:T(8,128)(2,1)S(1)} %pad_maximum_fusion.kv0), custom_call_target="tpu_custom_call" | custom-call | flops 15000000512 | bytes 1048576 | tf_op jit(solution)/shard_map/pallas_call | solution.py:136
  60.2 0.0 copy-done.7
  60.2 0.0 copy-done.5
  60.2 0.0 collective-permute-done.4.g3.refs_3_
  60.2 0.0 copy-done.1
  60.3 5.9 %shard_map.86 = bf16[3840,512]{1,0:T(8,128)(2,1)} custom-call(s32[4]{0:T(128)S(1)} %pad_add_fusion.place, bf16[512,512]{1,0:T(8,128)(2,1)S(1)} %shard_map.85.att_ref, bf16[128,3840]{1,0:T(8,128)(2,1)S(1)} %copy-done, bf16[128,3840]{1,0:T(8,128)(2,1)S(1)} %collective-permute-done.3.g1.refs_1_, bf16[128,3840]{1,0:T(8,128)(2,1)S(1)} %collective-permute-done.g2.refs_2_, ...), custom_call_target="tpu_custom_call" | custom-call | flops 20000000000 | bytes 1048576 | tf_op jit(solution)/shard_map/pallas_call | solution.py:171
  66.2 0.0 copy-start.2
  66.2 0.9 copy-done.2
  67.2 0.9 copy-done.9
  68.0 0.0 reduce-scatter.2.cloned.1.call-update
  68.0 0.0 copy-start.4
  68.0 18.2 %all-gather.2.cloned.1.call-done.refs_4_ = bf16[3840,512]{1,0:T(8,128)(2,1)} async-done(((bf16[480,512]{1,0:T(8,128)(2,1)}), bf16[3840,512]{1,0:T(8,128)(2,1)}) %all-gather.2.cloned.1.call-update) | async-done | bytes 3932176 | tf_op jit(solution)/shard_map/all_gather | solution.py:279
  86.3 1.0 copy-done.6
  87.3 1.0 copy-done.8
  88.3 1.0 copy-done.10
  89.4 14.2 %shard_map.87 = (f32[512,512]{1,0:T(8,128)}, bf16[512,512]{1,0:T(8,128)(2,1)S(1)}, bf16[512,512]{1,0:T(8,128)(2,1)S(1)}, f32[512,512]{1,0:T(8,128)}) custom-call(s32[4]{0:T(128)S(1)} %pad_add_fusion.place, bf16[512,512]{1,0:T(8,128)(2,1)S(1)} %copy-done.8, bf16[512,512]{1,0:T(8,128)(2,1)S(1)} %copy-done.10, bf16[512,512]{1,0:T(8,128)(2,1)S(1)} %copy-done.6, ...), custom_call_target="tpu_custom_call" | custom-call | flops 24999999488 | bytes 1048576 | tf_op jit(solution)/shard_map/pallas_call | solution.py:234
  103.6 1.3 collective-permute-start.5
  104.9 14.3 %collective-permute-done.5 = bf16[512,512]{1,0:T(8,128)(2,1)S(1)} collective-permute-done((bf16[512,512]{1,0:T(8,128)(2,1)S(1)}, bf16[512,512]{1,0:T(8,128)(2,1)S(1)}, u32[]{:S(2)}, u32[]{:S(2)}) %collective-permute-start.5) | collective-permute-done | bytes 524320 | tf_op jit(solution)/shard_map/ppermute | solution.py:47
  119.2 0.9 add_convert_fusion
  120.1 1.3 collective-permute-start.6
  121.4 44.5 %reduce-scatter.2.cloned.1.call-done = bf16[480,512]{1,0:T(8,128)(2,1)} async-done(((bf16[3840,512]{1,0:T(8,128)(2,1)}), bf16[480,512]{1,0:T(8,128)(2,1)}) %reduce-scatter.2.cloned.1.call-update) | async-done | bytes 491536 | tf_op jit(solution)/shard_map/reduce_scatter | solution.py:286
  165.9 1.9 %reshape.27 = bf16[8,60,512]{2,1,0:T(8,128)(2,1)} reshape(bf16[480,512]{1,0:T(8,128)(2,1)} %reduce-scatter.2.cloned.1.call-done) | data formatting | bytes 983040 | tf_op jit(solution)/shard_map/reshape | solution.py:293
  167.8 3.5 %all-to-all-start.1 = ((bf16[8,60,512]{2,1,0:T(8,128)(2,1)}), bf16[8,60,512]{2,1,0:T(8,128)(2,1)S(1)}, u32[]{:S(2)}, u32[]{:S(2)}) async-start(bf16[8,60,512]{2,1,0:T(8,128)(2,1)} %reshape.27), calls=%async_computation.2 | async-start | bytes 1048576 | tf_op jit(solution)/shard_map/all_to_all | solution.py:257
  171.3 0.0 copy-done.4
  171.3 0.0 copy-start.11
  171.3 1.2 copy-done.11
  172.6 1.2 shard_map.88
  173.8 8.5 %all-to-all-done.1 = bf16[8,60,512]{2,1,0:T(8,128)(2,1)S(1)} async-done(((bf16[8,60,512]{2,1,0:T(8,128)(2,1)}), bf16[8,60,512]{2,1,0:T(8,128)(2,1)S(1)}, u32[]{:S(2)}, u32[]{:S(2)}) %all-to-all-start.1) | async-done | bytes 491552 | tf_op jit(solution)/shard_map/all_to_all | solution.py:257
  182.3 0.7 convert_reduce_fusion
  183.0 0.0 collective-permute-done.6
  183.0 0.0 copy-done.13
  183.0 0.2 convert_add_fusion
  183.2 0.0 copy-done.12
  183.2 0.2 fusion.3
  183.4 0.7 slice.14
  184.2 0.9 fusion.6
  (12 shorter events, 0.0 us)
Async XLA Ops:
  7.2 23.2 %copy-start = (bf16[128,3840]{1,0:T(8,128)(2,1)S(1)}, bf16[128,3840]{1,0:T(8,128)(2,1)}, u32[]{:S(2)}) copy-start(bf16[128,3840]{1,0:T(8,128)(2,1)} %refs_0_.1) | copy-start | bytes 2949124
  7.2 20.3 %collective-permute-start = (bf16[128,3840]{1,0:T(8,128)(2,1)}, bf16[128,3840]{1,0:T(8,128)(2,1)S(1)}, u32[]{:S(2)}, u32[]{:S(2)}) collective-permute-start(bf16[128,3840]{1,0:T(8,128)(2,1)} %refs_0_.1), channel_id=1, source_target_pairs={{0,1},{1,0},{2,3},{3,2},{4,5},{5,4},{6,7},{7,6},{8,9},{9,8},{10,11... | collective-permute-start | bytes 2949128 | tf_op jit(solution)/shard_map/ppermute | solution.py:41
  9.0 17.6 %all-to-all-start = ((bf16[8,60,512]{2,1,0:T(8,128)(2,1)}), bf16[8,60,512]{2,1,0:T(8,128)(2,1)S(1)}, u32[]{:S(2)}, u32[]{:S(2)}) async-start(bf16[8,60,512]{2,1,0:T(8,128)(2,1)} %broadcast_in_dim.2), calls=%async_computation | async-start | bytes 1048576 | tf_op jit(solution)/shard_map/all_to_all | solution.py:272
  15.0 71.2 %all-gather.2.cloned.1.call-start = ((), (), s32[]{:S(2)}) async-start(), calls=%async_computation.3 | async-start | bytes 4423680 | tf_op jit(solution)/shard_map/all_gather | solution.py:279
  16.2 0.6 copy-start.14
  27.5 32.8 %copy-start.1 = (bf16[128,3840]{1,0:T(8,128)(2,1)}, bf16[128,3840]{1,0:T(8,128)(2,1)S(1)}, u32[]{:S(2)}) copy-start(bf16[128,3840]{1,0:T(8,128)(2,1)S(1)} %collective-permute-done.g2.refs_2_) | copy-start | bytes 2949124
  27.5 12.6 %collective-permute-start.1 = (bf16[512,512]{1,0:T(8,128)(2,1)S(1)}, bf16[512,512]{1,0:T(8,128)(2,1)}, u32[]{:S(2)}, u32[]{:S(2)}) collective-permute-start(bf16[512,512]{1,0:T(8,128)(2,1)S(1)} %pad_maximum_fusion.kv0), channel_id=1, source_target_pairs={{0,4},{4,8},{8,12},{12,16},{16,20},{20,24},{24,28},{28,32},{32,36}... | collective-permute-start | bytes 1572872 | tf_op jit(solution)/shard_map/ppermute | solution.py:47
  30.3 135.6 %reduce-scatter.2.cloned.1.call-start = ((), (), s32[]{:S(2)}) async-start(), calls=%async_computation.4 | async-start | bytes 4423680 | tf_op jit(solution)/shard_map/reduce_scatter | solution.py:286
  30.4 22.8 %collective-permute-start.3 = (bf16[128,3840]{1,0:T(8,128)(2,1)S(1)}, bf16[128,3840]{1,0:T(8,128)(2,1)S(1)}, u32[]{:S(2)}, u32[]{:S(2)}) collective-permute-start(bf16[128,3840]{1,0:T(8,128)(2,1)S(1)} %copy-done), channel_id=1, source_target_pairs={{0,2},{2,0},{1,3},{3,1},{4,6},{6,4},{5,7},{7,5},{8,10},{10,8},{9,1... | collective-permute-start | bytes 2949128 | tf_op jit(solution)/shard_map/ppermute | solution.py:41
  40.1 14.5 %collective-permute-start.2 = (bf16[512,512]{1,0:T(8,128)(2,1)}, bf16[512,512]{1,0:T(8,128)(2,1)S(1)}, u32[]{:S(2)}, u32[]{:S(2)}) collective-permute-start(bf16[512,512]{1,0:T(8,128)(2,1)} %collective-permute-done.1.kv1), channel_id=1, source_target_pairs={{0,4},{4,8},{8,12},{12,16},{16,20},{20,24},{24,28},{28,32},{32,36}... | collective-permute-start | bytes 1572872 | tf_op jit(solution)/shard_map/ppermute | solution.py:47
  44.6 1.1 copy-start.3
  45.9 14.3 %copy-start.7 = (bf16[512,512]{1,0:T(8,128)(2,1)}, bf16[512,512]{1,0:T(8,128)(2,1)S(1)}, u32[]{:S(2)}) copy-start(bf16[512,512]{1,0:T(8,128)(2,1)S(1)} %shard_map.84.q_ref) | copy-start | bytes 1572868
  54.6 5.7 %copy-start.5 = (bf16[512,512]{1,0:T(8,128)(2,1)}, bf16[512,512]{1,0:T(8,128)(2,1)S(1)}, u32[]{:S(2)}) copy-start(bf16[512,512]{1,0:T(8,128)(2,1)S(1)} %collective-permute-done.2.kv2) | copy-start | bytes 1572868
  54.6 5.7 %collective-permute-start.4 = (bf16[128,3840]{1,0:T(8,128)(2,1)S(1)}, bf16[128,3840]{1,0:T(8,128)(2,1)S(1)}, u32[]{:S(2)}, u32[]{:S(2)}) collective-permute-start(bf16[128,3840]{1,0:T(8,128)(2,1)S(1)} %collective-permute-done.3.g1.refs_1_), channel_id=1, source_target_pairs={{0,1},{1,0},{2,3},{3,2},{4,5},{5,4},{6,7},{7,6},{8,9},{9,8},{10,11... | collective-permute-start | bytes 2949128 | tf_op jit(solution)/shard_map/ppermute | solution.py:41
  66.2 0.9 copy-start.2
  67.2 0.9 copy-start.9
  68.0 103.3 %copy-start.4 = (bf16[512,512]{1,0:T(8,128)(2,1)S(1)}, bf16[512,512]{1,0:T(8,128)(2,1)}, u32[]{:S(2)}) copy-start(bf16[512,512]{1,0:T(8,128)(2,1)} %q_ref.1) | copy-start | bytes 1572868
  86.3 1.0 copy-start.6
  87.3 1.0 copy-start.8
  88.3 1.0 copy-start.10
  103.6 15.6 %collective-permute-start.5 = (bf16[512,512]{1,0:T(8,128)(2,1)S(1)}, bf16[512,512]{1,0:T(8,128)(2,1)S(1)}, u32[]{:S(2)}, u32[]{:S(2)}) collective-permute-start(bf16[512,512]{1,0:T(8,128)(2,1)S(1)} %get-tuple-element.27), channel_id=1, source_target_pairs={{4,0},{8,4},{12,8},{16,12},{20,16},{24,20},{28,24},{32,28},{36,32}... | collective-permute-start | bytes 1572872 | tf_op jit(solution)/shard_map/ppermute | solution.py:47
  120.1 62.9 %collective-permute-start.6 = (bf16[512,512]{1,0:T(8,128)(2,1)}, bf16[512,512]{1,0:T(8,128)(2,1)S(1)}, u32[]{:S(2)}, u32[]{:S(2)}) collective-permute-start(bf16[512,512]{1,0:T(8,128)(2,1)} %add_convert_fusion), channel_id=1, source_target_pairs={{4,0},{8,4},{12,8},{16,12},{20,16},{24,20},{28,24},{32,28},{36,32}... | collective-permute-start | bytes 1572872 | tf_op jit(solution)/shard_map/ppermute | solution.py:47
  167.8 14.5 %all-to-all-start.1 = ((bf16[8,60,512]{2,1,0:T(8,128)(2,1)}), bf16[8,60,512]{2,1,0:T(8,128)(2,1)S(1)}, u32[]{:S(2)}, u32[]{:S(2)}) async-start(bf16[8,60,512]{2,1,0:T(8,128)(2,1)} %reshape.27), calls=%async_computation.2 | async-start | bytes 1048576 | tf_op jit(solution)/shard_map/all_to_all | solution.py:257
  171.3 1.2 copy-start.11
  172.6 10.5 %copy-start.13 = (f32[512,512]{1,0:T(8,128)S(1)}, f32[512,512]{1,0:T(8,128)}, u32[]{:S(2)}) copy-start(f32[512,512]{1,0:T(8,128)} %get-tuple-element.26) | copy-start | bytes 3145732
  172.6 10.6 %copy-start.12 = (bf16[512,256]{1,0:T(8,128)(2,1)S(1)}, bf16[512,256]{1,0:T(8,128)(2,1)}, u32[]{:S(2)}) copy-start(bf16[512,256]{1,0:T(8,128)(2,1)} %param.6) | copy-start | bytes 786436
  172.6 10.6 %copy-start.15 = (f32[512]{0:T(512)S(1)}, f32[512]{0:T(512)}, u32[]{:S(2)}) copy-start(f32[512]{0:T(512)} %copy-done.14) | copy-start | bytes 6148
Sparse Core Ops, SparseCore 0:
  30.5 55.7 all-gather.1
  88.8 77.0 reduce-scatter.1

commit v2 on v1

--- a/solution.py
+++ b/solution.py
@@ -156,24 +156,37 @@
     ]
 
 
-def weight_kernel(place, att_ref, g0, g1, g2, g3, out_ref, grad, sems):
+def weight_kernel(place, att_ref, g0, g1, g2, g3, left_ref, right_ref, grad, right, sems):
     copies = copy_all(grad_rows(place, (g0, g1, g2, g3), grad), sems)
     for copy in copies:
         copy.wait()
     tile = HEAD_SIZE
     for n in range(grad.shape[1] // tile):
         part = contract(grad[:, n * tile : (n + 1) * tile], att_ref[...], 0, 0)
-        out_ref[n * tile : (n + 1) * tile, :] = part.astype(BF16)
+        left_ref[n * tile : (n + 1) * tile, :] = part[:, :HEAD_SIZE].astype(BF16)
+        right[n * tile : (n + 1) * tile, :] = part[:, HEAD_SIZE:]
+    inner, outer, rows, _ = right_ref.shape
+    for n in range(outer):
+        for y in range(inner):
+            first = (n * inner + y) * rows
+            right_ref[y, n] = right[first : first + rows, :].astype(BF16)
 
 
 def weight_partials(place, attended, grads):
     width = grads[0].shape[1]
     return pl.pallas_call(
         weight_kernel,
-        out_shape=jax.ShapeDtypeStruct((width, HEADS * HEAD_SIZE), BF16),
+        out_shape=(
+            jax.ShapeDtypeStruct((width, HEAD_SIZE), BF16),
+            jax.ShapeDtypeStruct((4, 16, width // 64, HEAD_SIZE), BF16),
+        ),
         in_specs=[SMEM, VMEM] + [ANY] * 4,
-        out_specs=VMEM,
-        scratch_shapes=[pltpu.VMEM((SPAN, width), BF16), pltpu.SemaphoreType.DMA((4,))],
+        out_specs=(VMEM, VMEM),
+        scratch_shapes=[
+            pltpu.VMEM((SPAN, width), BF16),
+            pltpu.VMEM((width, HEAD_SIZE), F32),
+            pltpu.SemaphoreType.DMA((4,)),
+        ],
         **params(20),
     )(place, attended, *grads)
 
@@ -271,28 +284,32 @@
     spread = jnp.broadcast_to(output_weight, (8,) + output_weight.shape)
     piece = lax.all_to_all(spread, ("xh", "y"), 0, 0).reshape(8 * rows, -1)
     core_grad, xl_source, piece = after((core_grad, output_grad, piece), piece, core_grad)
-    own_keys, query_raw = after((own_keys, query_raw), piece)
+    q_norm = norm_queries(after(query_raw, piece))
+    own_keys = after(own_keys, q_norm)
     xl_grad = shift(xl_source, "xl", 1)
-    behind = from_behind(own_keys, 1)
-    keys = [from_behind(behind, 1), behind, own_keys]
-    xl_grad = after(xl_grad, keys[0])
+    keys = [from_behind(own_keys, 2), from_behind(own_keys, 1), own_keys]
     weight = lax.all_gather(piece, "z", axis=0, tiled=True)
-    q_norm = norm_queries(query_raw)
     core_xl_grad = shift(xl_grad, "core", 1)
     attended = attend(place, q_norm, *keys)
     grads = [output_grad, xl_grad, core_grad, core_xl_grad]
-    partial = weight_partials(place, attended, grads)
-    weight, q_norm = after((weight, q_norm), partial)
-    partial = lax.psum_scatter(partial, "z", scatter_dimension=0, tiled=True)
+    left, right = weight_partials(place, attended, grads)
+    y = lax.axis_index("y")
+    sent = [lax.dynamic_index_in_dim(right, (y + k) % 4, 0, keepdims=False) for k in range(4)]
+    got = [shift(sent[k], "y", k) for k in (1, 2, 3)]
+    weight, q_norm = after((weight, q_norm), left, sent)
+    left = lax.psum_scatter(left, "z", scatter_dimension=0, tiled=True)
     query_sum, far, close, own = backward(
         place, q_norm, attended, keys, grads, [weight]
     )
-    passed_on = from_behind(far, -1).astype(F32) + close.astype(F32)
-    passed_on = from_behind(passed_on.astype(BF16), -1)
+    far_got, close_got = from_behind(far, -2), from_behind(close, -1)
     query_grad = finish_queries(query_sum, query_raw)
-    weight_grad = scatter(partial.reshape(8, rows, -1), ("xh", "y"))
-    passed_on = after(passed_on, weight_grad)
-    combined = own + passed_on.astype(F32)
+    got = after(got, query_grad)
+    right = sum((part.astype(F32) for part in got), sent[0].astype(F32))
+    right = scatter(right, ("z", "xh"))
+    left = scatter(after(left, right).reshape(8, rows, -1), ("xh", "y"))
+    weight_grad = jnp.concatenate([left, right], 1)
+    far_got, close_got = after((far_got, close_got), weight_grad)
+    combined = own + close_got.astype(F32) + far_got.astype(F32)
     key_raw_gradient = normalized_backward(combined[:, :HEAD_SIZE], key_unit, key_factor).astype(BF16)
     value_rows_gradient = combined[:, HEAD_SIZE:].astype(BF16)
     return (query_grad, key_raw_gradient, value_rows_gradient, weight_grad)

time: 194 us -> 193 us (level)
  waiting for transfers between devices: 110 us -> 50.6 us
  starting transfers between devices: 21 us -> 54.8 us
  blocking collectives: 0 us -> 20.4 us
  other arithmetic: 6.21 us -> 8.15 us
    reduce_scatter x1, waiting for transfers between devices: 44.5 us -> 0.02 us  [body(): left = lax.psum_scatter(left, 'z', scatter_dimension=0, tiled=True)]
    ppermute x3 -> x6, starting transfers between devices: 1.57 us -> 26.2 us  [shift(): lax.ppermute(block, axis, [(i, (i + distance) % size) for i in range(size)])]
    all_to_all x0 -> x1, blocking collectives: none -> 20.4 us  [scatter(): got = lax.all_to_all(pieces.astype(BF16), axes, 0, 0)]
    ppermute x4, waiting for transfers between devices: 23.9 us -> 4.78 us  [from_behind(): return lax.ppermute(block, CTX, route)]
    all_gather x1, waiting for transfers between devices: 18.2 us -> 0.02 us  [body(): weight = lax.all_gather(piece, 'z', axis=0, tiled=True)]
    all_to_all x1, waiting for transfers between devices: 8.51 us -> 20.3 us  [scatter(): got = lax.all_to_all(pieces.astype(BF16), axes, 0, 0)]
    all_to_all x1, starting transfers between devices: 3.49 us -> 12.5 us  [scatter(): got = lax.all_to_all(pieces.astype(BF16), axes, 0, 0)]
    ppermute x3 -> x6, waiting for transfers between devices: 7.24 us -> 16.2 us  [shift(): lax.ppermute(block, axis, [(i, (i + distance) % size) for i in range(size)])]
  transfers between devices with their start and end apart: 11 -> 14, of which waited for: 8 -> 6; matrix products, arithmetic and copies ran while one was open for 5% -> 6% of each run, Pallas kernels for 14% -> 15%
where the time goes in v2:
time: 193 us; the launch traced here: 190 us
  starting transfers between devices  54.8 us (28%)
  waiting for transfers between devices  50.6 us (26%)
  Pallas kernels  27.7 us (14%)
  blocking collectives  20.4 us (11%)
  between operations  14.3 us (7%)
  local copies, waits for them, and re-layouts  13.7 us (7%)
  other arithmetic  8.15 us (4%)
    ppermute x6, starting transfers between devices, shift(): lax.ppermute(block, axis, [(i, (i + distance) % size) for i in range(size)])  26.2 us
    all_to_all x1, blocking collectives, scatter(): got = lax.all_to_all(pieces.astype(BF16), axes, 0, 0)  20.4 us
    all_to_all x1, waiting for transfers between devices, scatter(): got = lax.all_to_all(pieces.astype(BF16), axes, 0, 0)  20.3 us
    ppermute x6, waiting for transfers between devices, shift(): lax.ppermute(block, axis, [(i, (i + distance) % size) for i in range(size)])  16.2 us
    pallas_call x1, Pallas kernels, backward(): pl.pallas_call(functools.partial(backward_kernel, len(parts)), out_shape=...  14.4 us
    all_to_all x1, starting transfers between devices, scatter(): got = lax.all_to_all(pieces.astype(BF16), axes, 0, 0)  12.5 us
    ppermute x4, starting transfers between devices, from_behind(): return lax.ppermute(block, CTX, route)  9.92 us
    all_to_all x1, waiting for transfers between devices, body(): piece = lax.all_to_all(spread, ('xh', 'y'), 0, 0).reshape(8 * rows, -1)  9.27 us
  transfers between devices with their start and end apart: 14, of which 6 were waited for; matrix products, arithmetic and copies ran while one was open for 6% of the time, Pallas kernels for 15%

profile of v2, /device:TPU:2, one launch (start us, length us, event | category | flops | bytes accessed | tf_op | source)
XLA Modules:
  0.0 189.7 jit_solution(18009053495720176434)
XLA Ops:
  7.2 0.1 collective-permute-start
  7.3 1.7 broadcast_in_dim.2
  9.0 6.2 %all-to-all-start = ((bf16[8,60,512]{2,1,0:T(8,128)(2,1)}), bf16[8,60,512]{2,1,0:T(8,128)(2,1)S(1)}, u32[]{:S(2)}, u32[]{:S(2)}) async-start(bf16[8,60,512]{2,1,0:T(8,128)(2,1)} %broadcast_in_dim.2), calls=%async_computation | async-start | bytes 1048576 | tf_op jit(solution)/shard_map/all_to_all | solution.py:285
  15.1 0.0 all-gather.2.cloned.1.call-start
  15.2 1.1 fusion.7
  16.3 0.0 copy-start.17
  16.3 1.1 fusion.2
  17.4 0.0 copy-done.16
  17.4 9.3 %all-to-all-done = bf16[8,60,512]{2,1,0:T(8,128)(2,1)S(1)} async-done(((bf16[8,60,512]{2,1,0:T(8,128)(2,1)}), bf16[8,60,512]{2,1,0:T(8,128)(2,1)S(1)}, u32[]{:S(2)}, u32[]{:S(2)}) %all-to-all-start) | async-done | bytes 491552 | tf_op jit(solution)/shard_map/all_to_all | solution.py:285
  26.7 0.9 reshape.26
  27.6 0.0 collective-permute-done.g2.refs_2_
  27.6 0.0 all-gather.2.cloned.1.call-update
  27.6 0.0 reduce-scatter.2.cloned.1.call-start
  27.7 1.5 collective-permute-start.3
  29.2 1.0 copy-done.3
  30.2 0.2 shard_map.84.q_ref
  30.5 0.0 copy-start.7
  30.5 0.8 copy-done.7
  31.2 2.8 %collective-permute-start.2 = (bf16[512,512]{1,0:T(8,128)(2,1)S(1)}, bf16[512,512]{1,0:T(8,128)(2,1)}, u32[]{:S(2)}, u32[]{:S(2)}) collective-permute-start(bf16[512,512]{1,0:T(8,128)(2,1)S(1)} %pad_maximum_fusion.kv0), channel_id=1, source_target_pairs={{0,4},{4,8},{8,12},{12,16},{16,20},{20,24},{24,28},{28,32},{32,36}... | collective-permute-start | bytes 1572872 | tf_op jit(solution)/shard_map/ppermute | solution.py:47
  34.0 4.6 %collective-permute-start.1 = (bf16[512,512]{1,0:T(8,128)(2,1)S(1)}, bf16[512,512]{1,0:T(8,128)(2,1)}, u32[]{:S(2)}, u32[]{:S(2)}) collective-permute-start(bf16[512,512]{1,0:T(8,128)(2,1)S(1)} %pad_maximum_fusion.kv0), channel_id=1, source_target_pairs={{0,8},{4,12},{8,16},{12,20},{16,24},{20,28},{24,32},{28,36},{32,40... | collective-permute-start | bytes 1572872 | tf_op jit(solution)/shard_map/ppermute | solution.py:47
  38.6 0.1 pad_add_fusion.place
  38.7 11.4 %collective-permute-done.3.g1.refs_1_ = bf16[128,3840]{1,0:T(8,128)(2,1)S(1)} collective-permute-done((bf16[128,3840]{1,0:T(8,128)(2,1)S(1)}, bf16[128,3840]{1,0:T(8,128)(2,1)S(1)}, u32[]{:S(2)}, u32[]{:S(2)}) %collective-permute-start.3) | collective-permute-done | bytes 983072 | tf_op jit(solution)/shard_map/ppermute | solution.py:41
  50.1 0.0 collective-permute-start.4
  50.1 0.0 collective-permute-done.2.kv1
  50.1 4.8 %collective-permute-done.1.kv2 = bf16[512,512]{1,0:T(8,128)(2,1)} collective-permute-done((bf16[512,512]{1,0:T(8,128)(2,1)S(1)}, bf16[512,512]{1,0:T(8,128)(2,1)}, u32[]{:S(2)}, u32[]{:S(2)}) %collective-permute-start.1) | collective-permute-done | bytes 524320 | tf_op jit(solution)/shard_map/ppermute | solution.py:47
  54.9 1.0 copy-done.8
  55.9 5.8 %shard_map.85.att_ref = bf16[512,512]{1,0:T(8,128)(2,1)S(1)} custom-call(s32[4]{0:T(128)S(1)} %pad_add_fusion.place, bf16[512,512]{1,0:T(8,128)(2,1)S(1)} %copy-done.8, bf16[512,512]{1,0:T(8,128)(2,1)} %collective-permute-done.1.kv2, bf16[512,512]{1,0:T(8,128)(2,1)} %collective-permute-done.2.kv1, bf16[512,512]{1,0:T(8,128)(2,1)S(1)} %pad_maximum_fusion.kv0), custom_call_target="tpu_custom_call" | custom-call | flops 15000000512 | bytes 1048576 | tf_op jit(solution)/shard_map/pallas_call | solution.py:136
  61.7 0.0 collective-permute-done.4.g3.refs_3_
  61.7 6.1 %shard_map.86 = (bf16[3840,256]{1,0:T(8,128)(2,1)}, bf16[4,16,60,256]{3,2,1,0:T(8,128)(2,1)}) custom-call(s32[4]{0:T(128)S(1)} %pad_add_fusion.place, bf16[512,512]{1,0:T(8,128)(2,1)S(1)} %shard_map.85.att_ref, bf16[128,3840]{1,0:T(8,128)(2,1)S(1)} %copy-done, bf16[128,3840]{1,0:T(8,128)(2,1)S(1)} %collective-permute-done.3.g1.refs_1_, ...), custom_call_target="tpu_custom_call" | custom-call | flops 20000000000 | bytes 1048576 | tf_op jit(solution)/shard_map/pallas_call | solution.py:177
  67.9 2.9 %dynamic-slice_bitcast_fusion = (bf16[16,60,256]{2,1,0:T(8,128)(2,1)}, bf16[16,60,256]{2,1,0:T(8,128)(2,1)}, bf16[16,60,256]{2,1,0:T(8,128)(2,1)}, bf16[16,60,256]{2,1,0:T(8,128)(2,1)}) fusion(bf16[4,16,60,256]{3,2,1,0:T(8,128)(2,1)} %get-tuple-element.29, s32[]{:T(128)S(6)} %select_n.39, s32[]{:T(128)S(6)} %select_n.37, s32[]{:T(128)S(6)} %select_n.35, ...), kind=kLoop, calls=%fused_computation.16 | loop fusion | bytes 3932176 | tf_op jit(solution)/shard_map/jit(dynamic_index_in_dim)/squeeze | solution.py:297
  70.8 23.8 %collective-permute-start.9 = (bf16[16,60,256]{2,1,0:T(8,128)(2,1)}, bf16[16,60,256]{2,1,0:T(8,128)(2,1)}, u32[]{:S(2)}, u32[]{:S(2)}) collective-permute-start(bf16[16,60,256]{2,1,0:T(8,128)(2,1)} %get-tuple-element.42), channel_id=1, source_target_pairs={{0,12},{4,0},{8,4},{12,8},{1,13},{5,1},{9,5},{13,9},{2,14},{6,2},{... | collective-permute-start | bytes 1474568 | tf_op jit(solution)/shard_map/ppermute | solution.py:41
  94.6 0.0 collective-permute-start.8
  94.6 0.9 collective-permute-start.7
  95.5 0.0 reduce-scatter.2.cloned.1.call-update
  95.5 0.0 all-gather.2.cloned.1.call-done.refs_4_
  95.5 0.0 copy-start.9
  95.5 1.0 copy-done.9
  96.6 1.0 copy-done.11
  97.6 14.4 %shard_map.87 = (f32[512,512]{1,0:T(8,128)}, bf16[512,512]{1,0:T(8,128)(2,1)S(1)}, bf16[512,512]{1,0:T(8,128)(2,1)S(1)}, f32[512,512]{1,0:T(8,128)}) custom-call(s32[4]{0:T(128)S(1)} %pad_add_fusion.place, bf16[512,512]{1,0:T(8,128)(2,1)S(1)} %copy-done.9, bf16[512,512]{1,0:T(8,128)(2,1)S(1)} %copy-done.11, bf16[512,512]{1,0:T(8,128)(2,1)} %collective-permute-done.1.kv2, ...), custom_call_target="tpu_custom_call" | custom-call | flops 24999999488 | bytes 1048576 | tf_op jit(solution)/shard_map/pallas_call | solution.py:247
  112.0 1.4 copy-done.12
  113.4 1.2 shard_map.88
  114.7 1.3 collective-permute-done.9
  116.0 0.0 collective-permute-done.8
  116.0 3.4 %collective-permute-done.7 = bf16[16,60,256]{2,1,0:T(8,128)(2,1)} collective-permute-done((bf16[16,60,256]{2,1,0:T(8,128)(2,1)}, bf16[16,60,256]{2,1,0:T(8,128)(2,1)}, u32[]{:S(2)}, u32[]{:S(2)}) %collective-permute-start.7) | collective-permute-done | bytes 491552 | tf_op jit(solution)/shard_map/ppermute | solution.py:41
  119.4 0.0 copy-done.14
  119.4 2.5 %add_convert_fusion = bf16[16,60,256]{2,1,0:T(8,128)(2,1)} fusion(bf16[16,60,256]{2,1,0:T(8,128)(2,1)} %collective-permute-done.9, bf16[16,60,256]{2,1,0:T(8,128)(2,1)} %collective-permute-done.8, bf16[16,60,256]{2,1,0:T(8,128)(2,1)} %collective-permute-done.7, bf16[16,60,256]{2,1,0:T(8,128)(2,1)S(1)} %copy-done.14), kind=kLoop, calls=%fused_computation.2 | loop fusion | flops 1966080 | bytes 2457600 | tf_op jit(solution)/shard_map/convert_element_type | solution.py:270
  121.9 12.5 %all-to-all-start.1 = ((bf16[16,60,256]{2,1,0:T(8,128)(2,1)}), bf16[16,60,256]{2,1,0:T(8,128)(2,1)S(1)}, u32[]{:S(2)}, u32[]{:S(2)}) async-start(bf16[16,60,256]{2,1,0:T(8,128)(2,1)} %add_convert_fusion), calls=%async_computation.2 | async-start | bytes 1048576 | tf_op jit(solution)/shard_map/all_to_all | solution.py:270
  134.4 1.3 collective-permute-start.5
  135.7 1.3 collective-permute-start.6
  137.0 20.3 %all-to-all-done.1 = bf16[16,60,256]{2,1,0:T(8,128)(2,1)S(1)} async-done(((bf16[16,60,256]{2,1,0:T(8,128)(2,1)}), bf16[16,60,256]{2,1,0:T(8,128)(2,1)S(1)}, u32[]{:S(2)}, u32[]{:S(2)}) %all-to-all-start.1) | async-done | bytes 491552 | tf_op jit(solution)/shard_map/all_to_all | solution.py:270
  157.3 0.1 convert_reduce_fusion
  157.4 0.0 reduce-scatter.2.cloned.1.call-done
  157.4 1.0 reshape.27
  158.4 0.0 copy-start.13
  158.4 0.0 copy-start.18
  158.4 20.4 %all_to_all.15 = bf16[8,60,256]{2,1,0:T(8,128)(2,1)S(1)} all-to-all(bf16[8,60,256]{2,1,0:T(8,128)(2,1)S(1)} %reshape.27), channel_id=1, replica_groups=mesh['z'=8,'xh'=2,'y'=4,'xl'=2,'core'=2] {'xh','y'}, dimensions={0} | all-to-all | bytes 491520 | tf_op jit(solution)/shard_map/all_to_all | solution.py:270
  178.9 0.7 pad_maximum_fusion.1
  179.6 0.0 collective-permute-done.5
  179.6 0.0 collective-permute-done.6
  179.6 0.0 copy-done.15
  179.6 1.4 convert_add_fusion
  181.0 0.2 fusion.3
  181.2 0.7 slice.14
  182.0 0.9 fusion.6
  (28 shorter events, 0.1 us)
Async XLA Ops:
  7.2 10.2 %copy-start.16 = (bf16[512,256]{1,0:T(8,128)(2,1)S(1)}, bf16[512,256]{1,0:T(8,128)(2,1)}, u32[]{:S(2)}) copy-start(bf16[512,256]{1,0:T(8,128)(2,1)} %param.7) | copy-start | bytes 786436
  7.2 20.4 %collective-permute-start = (bf16[128,3840]{1,0:T(8,128)(2,1)}, bf16[128,3840]{1,0:T(8,128)(2,1)S(1)}, u32[]{:S(2)}, u32[]{:S(2)}) collective-permute-start(bf16[128,3840]{1,0:T(8,128)(2,1)} %refs_0_.1), channel_id=1, source_target_pairs={{0,1},{1,0},{2,3},{3,2},{4,5},{5,4},{6,7},{7,6},{8,9},{9,8},{10,11... | collective-permute-start | bytes 2949128 | tf_op jit(solution)/shard_map/ppermute | solution.py:41
  9.0 18.7 %copy-start = (bf16[128,3840]{1,0:T(8,128)(2,1)S(1)}, bf16[128,3840]{1,0:T(8,128)(2,1)}, u32[]{:S(2)}) copy-start(bf16[128,3840]{1,0:T(8,128)(2,1)} %refs_0_.1) | copy-start | bytes 2949124
  9.0 17.8 %all-to-all-start = ((bf16[8,60,512]{2,1,0:T(8,128)(2,1)}), bf16[8,60,512]{2,1,0:T(8,128)(2,1)S(1)}, u32[]{:S(2)}, u32[]{:S(2)}) async-start(bf16[8,60,512]{2,1,0:T(8,128)(2,1)} %broadcast_in_dim.2), calls=%async_computation | async-start | bytes 1048576 | tf_op jit(solution)/shard_map/all_to_all | solution.py:285
  15.1 80.4 %all-gather.2.cloned.1.call-start = ((), (), s32[]{:S(2)}) async-start(), calls=%async_computation.4 | async-start | bytes 4423680 | tf_op jit(solution)/shard_map/all_gather | solution.py:291
  16.3 11.4 %copy-start.17 = (f32[512]{0:T(512)}, f32[512]{0:T(512)S(1)}, u32[]{:S(2)}) copy-start(f32[512]{0:T(512)S(1)} %add_rsqrt_fusion) | copy-start | bytes 6148
  27.6 34.1 %copy-start.1 = (bf16[128,3840]{1,0:T(8,128)(2,1)}, bf16[128,3840]{1,0:T(8,128)(2,1)S(1)}, u32[]{:S(2)}) copy-start(bf16[128,3840]{1,0:T(8,128)(2,1)S(1)} %collective-permute-done.g2.refs_2_) | copy-start | bytes 2949124
  27.6 129.7 %reduce-scatter.2.cloned.1.call-start = ((), (), s32[]{:S(2)}) async-start(), calls=%async_computation.5 | async-start | bytes 2211840 | tf_op jit(solution)/shard_map/reduce_scatter | solution.py:300
  27.7 22.4 %collective-permute-start.3 = (bf16[128,3840]{1,0:T(8,128)(2,1)S(1)}, bf16[128,3840]{1,0:T(8,128)(2,1)S(1)}, u32[]{:S(2)}, u32[]{:S(2)}) collective-permute-start(bf16[128,3840]{1,0:T(8,128)(2,1)S(1)} %copy-done), channel_id=1, source_target_pairs={{0,2},{2,0},{1,3},{3,1},{4,6},{6,4},{5,7},{7,5},{8,10},{10,8},{9,1... | collective-permute-start | bytes 2949128 | tf_op jit(solution)/shard_map/ppermute | solution.py:41
  29.2 1.0 copy-start.3
  30.5 0.8 copy-start.7
  31.2 18.9 %collective-permute-start.2 = (bf16[512,512]{1,0:T(8,128)(2,1)S(1)}, bf16[512,512]{1,0:T(8,128)(2,1)}, u32[]{:S(2)}, u32[]{:S(2)}) collective-permute-start(bf16[512,512]{1,0:T(8,128)(2,1)S(1)} %pad_maximum_fusion.kv0), channel_id=1, source_target_pairs={{0,4},{4,8},{8,12},{12,16},{16,20},{20,24},{24,28},{28,32},{32,36}... | collective-permute-start | bytes 1572872 | tf_op jit(solution)/shard_map/ppermute | solution.py:47
  34.0 20.9 %collective-permute-start.1 = (bf16[512,512]{1,0:T(8,128)(2,1)S(1)}, bf16[512,512]{1,0:T(8,128)(2,1)}, u32[]{:S(2)}, u32[]{:S(2)}) collective-permute-start(bf16[512,512]{1,0:T(8,128)(2,1)S(1)} %pad_maximum_fusion.kv0), channel_id=1, source_target_pairs={{0,8},{4,12},{8,16},{12,20},{16,24},{20,28},{24,32},{28,36},{32,40... | collective-permute-start | bytes 1572872 | tf_op jit(solution)/shard_map/ppermute | solution.py:47
  50.1 11.6 %collective-permute-start.4 = (bf16[128,3840]{1,0:T(8,128)(2,1)S(1)}, bf16[128,3840]{1,0:T(8,128)(2,1)S(1)}, u32[]{:S(2)}, u32[]{:S(2)}) collective-permute-start(bf16[128,3840]{1,0:T(8,128)(2,1)S(1)} %collective-permute-done.3.g1.refs_1_), channel_id=1, source_target_pairs={{0,1},{1,0},{2,3},{3,2},{4,5},{5,4},{6,7},{7,6},{8,9},{9,8},{10,11... | collective-permute-start | bytes 2949128 | tf_op jit(solution)/shard_map/ppermute | solution.py:41
  54.9 1.0 copy-start.8
  61.7 6.2 %copy-start.10 = (bf16[512,512]{1,0:T(8,128)(2,1)}, bf16[512,512]{1,0:T(8,128)(2,1)S(1)}, u32[]{:S(2)}) copy-start(bf16[512,512]{1,0:T(8,128)(2,1)S(1)} %shard_map.85.att_ref) | copy-start | bytes 1572868
  61.7 6.2 %copy-start.2 = (bf16[128,3840]{1,0:T(8,128)(2,1)}, bf16[128,3840]{1,0:T(8,128)(2,1)S(1)}, u32[]{:S(2)}) copy-start(bf16[128,3840]{1,0:T(8,128)(2,1)S(1)} %collective-permute-done.4.g3.refs_3_) | copy-start | bytes 2949124
  70.8 45.1 %collective-permute-start.9 = (bf16[16,60,256]{2,1,0:T(8,128)(2,1)}, bf16[16,60,256]{2,1,0:T(8,128)(2,1)}, u32[]{:S(2)}, u32[]{:S(2)}) collective-permute-start(bf16[16,60,256]{2,1,0:T(8,128)(2,1)} %get-tuple-element.42), channel_id=1, source_target_pairs={{0,12},{4,0},{8,4},{12,8},{1,13},{5,1},{9,5},{13,9},{2,14},{6,2},{... | collective-permute-start | bytes 1474568 | tf_op jit(solution)/shard_map/ppermute | solution.py:41
  94.6 21.4 %collective-permute-start.8 = (bf16[16,60,256]{2,1,0:T(8,128)(2,1)}, bf16[16,60,256]{2,1,0:T(8,128)(2,1)}, u32[]{:S(2)}, u32[]{:S(2)}) collective-permute-start(bf16[16,60,256]{2,1,0:T(8,128)(2,1)} %get-tuple-element.43), channel_id=1, source_target_pairs={{0,8},{4,12},{8,0},{12,4},{1,9},{5,13},{9,1},{13,5},{2,10},{6,14},... | collective-permute-start | bytes 1474568 | tf_op jit(solution)/shard_map/ppermute | solution.py:41
  94.6 24.8 %collective-permute-start.7 = (bf16[16,60,256]{2,1,0:T(8,128)(2,1)}, bf16[16,60,256]{2,1,0:T(8,128)(2,1)}, u32[]{:S(2)}, u32[]{:S(2)}) collective-permute-start(bf16[16,60,256]{2,1,0:T(8,128)(2,1)} %get-tuple-element.44), channel_id=1, source_target_pairs={{0,4},{4,8},{8,12},{12,0},{1,5},{5,9},{9,13},{13,1},{2,6},{6,10},{... | collective-permute-start | bytes 1474568 | tf_op jit(solution)/shard_map/ppermute | solution.py:41
  95.5 1.0 copy-start.9
  96.6 1.0 copy-start.11
  97.6 14.4 %copy-start.4 = (bf16[512,512]{1,0:T(8,128)(2,1)S(1)}, bf16[512,512]{1,0:T(8,128)(2,1)}, u32[]{:S(2)}) copy-start(bf16[512,512]{1,0:T(8,128)(2,1)} %q_ref.2) | copy-start | bytes 1572868
  112.0 2.7 %copy-start.5 = (bf16[512,512]{1,0:T(8,128)(2,1)}, bf16[512,512]{1,0:T(8,128)(2,1)S(1)}, u32[]{:S(2)}) copy-start(bf16[512,512]{1,0:T(8,128)(2,1)S(1)} %get-tuple-element.34) | copy-start | bytes 1572868
  112.0 1.4 copy-start.12
  113.4 6.0 %copy-start.14 = (bf16[16,60,256]{2,1,0:T(8,128)(2,1)S(1)}, bf16[16,60,256]{2,1,0:T(8,128)(2,1)}, u32[]{:S(2)}) copy-start(bf16[16,60,256]{2,1,0:T(8,128)(2,1)} %get-tuple-element.45) | copy-start | bytes 1474564
  116.0 18.4 %copy-start.6 = (bf16[512,512]{1,0:T(8,128)(2,1)S(1)}, bf16[512,512]{1,0:T(8,128)(2,1)}, u32[]{:S(2)}) copy-start(bf16[512,512]{1,0:T(8,128)(2,1)} %copy-done.5) | copy-start | bytes 1572868
  121.9 57.7 %copy-start.15 = (f32[512,512]{1,0:T(8,128)S(1)}, f32[512,512]{1,0:T(8,128)}, u32[]{:S(2)}) copy-start(f32[512,512]{1,0:T(8,128)} %get-tuple-element.33) | copy-start | bytes 3145732
  121.9 35.4 %all-to-all-start.1 = ((bf16[16,60,256]{2,1,0:T(8,128)(2,1)}), bf16[16,60,256]{2,1,0:T(8,128)(2,1)S(1)}, u32[]{:S(2)}, u32[]{:S(2)}) async-start(bf16[16,60,256]{2,1,0:T(8,128)(2,1)} %add_convert_fusion), calls=%async_computation.2 | async-start | bytes 1048576 | tf_op jit(solution)/shard_map/all_to_all | solution.py:270
  134.4 45.2 %collective-permute-start.5 = (bf16[512,512]{1,0:T(8,128)(2,1)S(1)}, bf16[512,512]{1,0:T(8,128)(2,1)}, u32[]{:S(2)}, u32[]{:S(2)}) collective-permute-start(bf16[512,512]{1,0:T(8,128)(2,1)S(1)} %copy-done.6), channel_id=1, source_target_pairs={{8,0},{12,4},{16,8},{20,12},{24,16},{28,20},{32,24},{36,28},{40,32... | collective-permute-start | bytes 1572872 | tf_op jit(solution)/shard_map/ppermute | solution.py:47
  135.7 43.9 %collective-permute-start.6 = (bf16[512,512]{1,0:T(8,128)(2,1)S(1)}, bf16[512,512]{1,0:T(8,128)(2,1)}, u32[]{:S(2)}, u32[]{:S(2)}) collective-permute-start(bf16[512,512]{1,0:T(8,128)(2,1)S(1)} %get-tuple-element.35), channel_id=1, source_target_pairs={{4,0},{8,4},{12,8},{16,12},{20,16},{24,20},{28,24},{32,28},{36,32}... | collective-permute-start | bytes 1572872 | tf_op jit(solution)/shard_map/ppermute | solution.py:47
  158.4 22.6 %copy-start.13 = (bf16[512,256]{1,0:T(8,128)(2,1)S(1)}, bf16[512,256]{1,0:T(8,128)(2,1)}, u32[]{:S(2)}) copy-start(bf16[512,256]{1,0:T(8,128)(2,1)} %param.6) | copy-start | bytes 786436
  158.4 22.6 %copy-start.18 = (f32[512]{0:T(512)S(1)}, f32[512]{0:T(512)}, u32[]{:S(2)}) copy-start(f32[512]{0:T(512)} %copy-done.17) | copy-start | bytes 6148
Sparse Core Ops, SparseCore 0:
  27.8 52.6 all-gather.1
  95.6 61.4 reduce-scatter.1
